TPU v7x, 512 devices: a whole 4x4x16 slice. The times are simulated.
512 devices in a mesh: rows: 128 (over x, z_lo, y), feat: 4 (over z_hi, core).
Axes of the slice: x: 4, y: 4, z: 16 (z_hi: 2, z_lo: 8; z = z_hi * 8 + z_lo), core: 2. Of those that a mesh axis runs over, the one named last changes fastest.
Arguments:
- features: bfloat16 [32768, 512], P('rows', 'feat'), may hold values from -6 to 6
- weight: bfloat16 [512, 512], P(None, 'feat'), may hold values from -0.25 to 0.25
- block_values: bfloat16 [256, 8, 128, 128], P('rows', 'feat'), may hold values from -0.25 to 0.25
- columns: int32 [256, 8], P('rows'), may hold values from 0 to 255, as said below
- counts: int32 [256], P('rows'), may hold values from 2 to 8, as said below
- cotangent: bfloat16 [32768, 512], P('rows', 'feat'), may hold values from -6 to 6
Outputs:
- hidden: bfloat16 [32768, 512], P('rows', 'feat')
- grad_features: bfloat16 [32768, 512], P('rows', 'feat')
- grad_weight: float32 [512, 512], P(None, 'feat')
Inputs may be any that keep to these rules, and one draw needn't show every extreme that they name: `columns`: the 8 column blocks of a row block are distinct and lie on the devices within 4 indices of the row block's own index along rows, counted around the axis (the device of block c is c // 2). Slots 0 to counts[g] - 1 of row block g are live, the others are ignored; some row block has exactly 8 live slots.
All inputs are finite; a program needn't handle non-finite values.
Results may differ from a plain program's by a relative error of at most 0.0067.
Values may be sent and summed in bfloat16 or wider, within the bound.
No kernel may reach another device: no remote copies, remote signals or barrier semaphores. Data moves between devices by JAX's collectives and lax.ppermute only.
A program may use at most 64 MiB of HBM per device.

v0:
```python
import jax
import jax.numpy as jnp
from jax import lax
from jax.sharding import PartitionSpec as P


def shifted(value, axis, steps):
    count = lax.axis_size(axis)
    pairs = [(source, (source + steps) % count) for source in range(count)]
    return lax.ppermute(value, axis, pairs)


def activation(values):
    return jax.nn.gelu(values, approximate=True)


def window_index(columns, row_blocks, center, halo_reach, row_count):
    owner_dev = columns // row_blocks
    offset = (owner_dev - center + halo_reach + row_count) % row_count
    return offset * row_blocks + columns % row_blocks


def live_tiles(panel_part, first_slot, counts, places):
    slot_count = panel_part.shape[1]
    slot_ids = first_slot + jnp.arange(slot_count)
    slot_live = counts[:, None] > slot_ids[None, :]
    tiles = jnp.where(slot_live[:, :, None, None], panel_part, jnp.zeros((), panel_part.dtype))
    return (tiles, places)


def gather_slots(panel_part, first_slot, counts, places, window):
    tiles, targets = live_tiles(panel_part, first_slot, counts, places)
    picked = jnp.take(window, targets, axis=0)
    product = jnp.einsum("gsij,gsjf->gif", tiles, picked, preferred_element_type=jnp.float32)
    return product


def spread_slots(running, panel_part, first_slot, counts, places, grad_blocks):
    tiles, targets = live_tiles(panel_part, first_slot, counts, places)
    block_size = grad_blocks.shape[1]
    feat_width = grad_blocks.shape[2]
    product = jnp.einsum("gsij,gif->gsjf", tiles, grad_blocks, preferred_element_type=jnp.float32)
    return running.at[targets.reshape(-1)].add(product.reshape(-1, block_size, feat_width))


def on_device(features, weight, block_values, columns, counts, cotangent):
    row_count = lax.axis_size("rows")
    center = lax.axis_index("rows")
    halo_reach = min(4, (row_count - 1) // 3)
    row_blocks = counts.shape[0]
    block_size = block_values.shape[2]
    feat_width = features.shape[1]
    local_rows = features.shape[0]
    span_blocks = (2 * halo_reach + 1) * row_blocks
    pieces = {0: features}
    for offset in list(range(-halo_reach, 0)) + list(range(1, halo_reach + 1)):
        pieces[offset] = shifted(features, "rows", -offset)
    window = jnp.stack([pieces[offset] for offset in range(-halo_reach, halo_reach + 1)])
    window = window.reshape(span_blocks, block_size, feat_width)
    places = window_index(columns, row_blocks, center, halo_reach, row_count)
    panel_full = lax.all_gather(block_values, "feat", axis=1, tiled=True)
    summed = gather_slots(panel_full, 0, counts, places, window)
    aggregated = summed.reshape(local_rows, feat_width).astype(jnp.bfloat16)
    agg_full, weight_full = (
        lax.all_gather(aggregated, "feat", axis=1, tiled=True),
        lax.all_gather(weight, "feat", axis=1, tiled=True),
    )
    pre_act = jnp.dot(agg_full, weight, preferred_element_type=jnp.float32)
    hidden, act_grad = jax.vjp(activation, pre_act)
    grad_pre = act_grad(cotangent.astype(jnp.float32))[0].astype(jnp.bfloat16)
    grad_full = lax.all_gather(grad_pre, "feat", axis=1, tiled=True)
    weight_terms = lax.dot_general(
        agg_full, grad_pre, (((0,), (0,)), ((), ())), preferred_element_type=jnp.float32
    )
    node_total = local_rows * row_count
    grad_weight = lax.psum(weight_terms, "rows") * float(node_total) ** (-0.5)
    feat_index = lax.axis_index("feat")
    weight_rows = lax.dynamic_slice_in_dim(weight_full, feat_index * feat_width, feat_width, 0)
    grad_agg = lax.dot_general(
        grad_full, weight_rows, (((1,), (1,)), ((), ())), preferred_element_type=jnp.float32
    )
    grad_blocks = grad_agg.astype(jnp.bfloat16).reshape(row_blocks, block_size, feat_width)
    zero_window = jnp.zeros((span_blocks, block_size, feat_width), jnp.float32)
    spread = spread_slots(zero_window, panel_full, 0, counts, places, grad_blocks)
    spread = spread.reshape(2 * halo_reach + 1, local_rows, feat_width)
    grad_local = spread[halo_reach]
    for offset in list(range(-halo_reach, 0)) + list(range(1, halo_reach + 1)):
        outgoing = spread[halo_reach + offset].astype(jnp.bfloat16)
        arrived = shifted(outgoing, "rows", offset)
        grad_local = grad_local + arrived.astype(jnp.float32)
    return (hidden.astype(jnp.bfloat16), grad_local.astype(jnp.bfloat16), grad_weight)


def solution(mesh):
    in_specs = (
        P("rows", "feat"),
        P(None, "feat"),
        P("rows", "feat", None, None),
        P("rows", None),
        P("rows"),
        P("rows", "feat"),
    )
    out_specs = (P("rows", "feat"), P("rows", "feat"), P(None, "feat"))
    return jax.shard_map(
        on_device, mesh=mesh, in_specs=in_specs, out_specs=out_specs, check_vma=False
    )
```

profile of v0, /device:TPU:0, one launch (start us, length us, event | category | flops | bytes accessed | tf_op | source)
XLA Modules:
  0.0 2029.0 jit_solution(9673792675788454822)
XLA Ops:
  7.2 0.0 copy-start.1
  7.2 0.0 all-reduce.2.cloned.1.call-start
  7.2 12.6 collective-permute-start.5
  19.9 3.0 collective-permute-start.4
  22.8 2.9 collective-permute-start.3
  25.7 2.6 collective-permute-start.2
  28.4 1.9 collective-permute-start
  30.3 0.7 compare_and_fusion
  31.0 0.1 reshape.102
  31.1 0.7 iota_compare_fusion
  31.8 0.1 reshape.107
  31.9 20.9 %all_gather.12 = bf16[2,8,128,128]{3,2,1,0:T(8,128)(2,1)S(1)} all-gather(bf16[2,2,128,128]{3,2,1,0:T(8,128)(2,1)} %param.8), channel_id=1, replica_groups=mesh['rows'=128,'feat'=4] {'feat'}, dimensions={1}, use_global_device_ids=true | all-gather | bytes 655360 | tf_op jit(solution)/shard_map/all_gather | solution.py:61
  52.8 20.9 %all_gather.15 = bf16[512,512]{1,0:T(8,128)(2,1)S(1)} all-gather(bf16[512,128]{1,0:T(8,128)(2,1)} %param.7), channel_id=1, replica_groups=mesh['rows'=128,'feat'=4] {'feat'}, dimensions={1}, use_global_device_ids=true | all-gather | bytes 655360 | tf_op jit(solution)/shard_map/all_gather | solution.py:66
  73.7 0.0 collective-permute-done
  73.7 0.0 copy-done.1
  73.7 1.9 collective-permute-start.1
  75.7 14.1 collective-permute-done.1
  89.7 1.9 collective-permute-start.7
  91.7 0.0 collective-permute-done.2
  91.7 2.0 collective-permute-start.6
  93.7 0.0 collective-permute-done.3
  93.7 0.0 collective-permute-done.4
  93.7 0.0 collective-permute-done.5
  93.8 5.3 collective-permute-done.6
  99.1 0.0 collective-permute-done.7
  99.1 0.6 gather_fusion
  99.8 0.0 copy-start
  99.8 0.0 copy-start.2
  99.8 0.4 fusion
  100.2 15.2 all_gather.13
  115.4 0.0 copy-done
  115.4 0.0 copy-done.2
  115.4 0.9 fusion.9
  116.3 14.6 all_gather.14
  130.9 0.2 convolution_convert_fusion
  131.2 0.4 fusion.3
  131.6 0.1 broadcast_in_dim.43
  131.7 1.6 scatter_fusion
  133.3 0.1 convert.10
  133.5 3.3 collective-permute-start.15
  136.8 11.3 collective-permute-start.8
  148.1 5.2 collective-permute-start.14
  153.2 3.1 collective-permute-start.13
  156.3 1.9 collective-permute-start.12
  158.2 0.0 collective-permute-done.15
  158.2 14.7 collective-permute-start.11
  173.0 0.0 collective-permute-done.8
  173.0 3.1 collective-permute-start.10
  176.1 0.0 collective-permute-done.14
  176.1 3.9 collective-permute-start.9
  180.0 1.0 fusion.36
  180.9 0.0 all-reduce.2.cloned.1.call-update
  181.0 0.0 collective-permute-done.13
  181.0 0.0 collective-permute-done.12
  181.0 0.0 collective-permute-done.11
  181.0 0.0 collective-permute-done.10
  181.0 2.4 collective-permute-done.9
  183.5 0.7 fusion.24
  184.2 1836.3 %all-reduce.2.cloned.1.call-done = f32[512,128]{1,0:T(8,128)} async-done(((f32[512,128]{1,0:T(8,128)}), f32[512,128]{1,0:T(8,128)}) %all-reduce.2.cloned.1.call-update) | async-done | bytes 262160 | tf_op jit(solution)/shard_map/psum | solution.py:76
  2020.5 1.7 broadcast_multiply_fusion
  (14 shorter events, 0.2 us)
Async XLA Ops:
  7.2 66.6 %copy-start.1 = (bf16[256,128]{1,0:T(8,128)(2,1)S(1)}, bf16[256,128]{1,0:T(8,128)(2,1)}, u32[]{:S(2)}) copy-start(bf16[256,128]{1,0:T(8,128)(2,1)} %param.6) | copy-start | bytes 196612
  7.2 2013.3 %all-reduce.2.cloned.1.call-start = ((), (), s32[]{:S(2)}) async-start(), calls=%async_computation | async-start | bytes 524288 | tf_op jit(solution)/shard_map/psum | solution.py:76
  7.2 86.5 %collective-permute-start.5 = (bf16[256,128]{1,0:T(8,128)(2,1)}, bf16[256,128]{1,0:T(8,128)(2,1)S(1)}, u32[]{:S(2)}, u32[]{:S(2)}) collective-permute-start(bf16[256,128]{1,0:T(8,128)(2,1)} %param.6), channel_id=1, source_target_pairs={{0,504},{4,508},{8,0},{12,4},{16,8},{20,12},{24,16},{28,20},{32,24... | collective-permute-start | bytes 196616 | tf_op jit(solution)/shard_map/ppermute | solution.py:10
  19.9 73.9 %collective-permute-start.4 = (bf16[256,128]{1,0:T(8,128)(2,1)}, bf16[256,128]{1,0:T(8,128)(2,1)S(1)}, u32[]{:S(2)}, u32[]{:S(2)}) collective-permute-start(bf16[256,128]{1,0:T(8,128)(2,1)} %param.6), channel_id=1, source_target_pairs={{0,508},{4,0},{8,4},{12,8},{16,12},{20,16},{24,20},{28,24},{32,28}... | collective-permute-start | bytes 196616 | tf_op jit(solution)/shard_map/ppermute | solution.py:10
  22.8 70.8 %collective-permute-start.3 = (bf16[256,128]{1,0:T(8,128)(2,1)}, bf16[256,128]{1,0:T(8,128)(2,1)S(1)}, u32[]{:S(2)}, u32[]{:S(2)}) collective-permute-start(bf16[256,128]{1,0:T(8,128)(2,1)} %param.6), channel_id=1, source_target_pairs={{0,4},{4,8},{8,12},{12,16},{16,20},{20,24},{24,28},{28,32},{32,36}... | collective-permute-start | bytes 196616 | tf_op jit(solution)/shard_map/ppermute | solution.py:10
  25.7 66.0 %collective-permute-start.2 = (bf16[256,128]{1,0:T(8,128)(2,1)}, bf16[256,128]{1,0:T(8,128)(2,1)S(1)}, u32[]{:S(2)}, u32[]{:S(2)}) collective-permute-start(bf16[256,128]{1,0:T(8,128)(2,1)} %param.6), channel_id=1, source_target_pairs={{0,8},{4,12},{8,16},{12,20},{16,24},{20,28},{24,32},{28,36},{32,40... | collective-permute-start | bytes 196616 | tf_op jit(solution)/shard_map/ppermute | solution.py:10
  28.4 45.4 %collective-permute-start = (bf16[256,128]{1,0:T(8,128)(2,1)}, bf16[256,128]{1,0:T(8,128)(2,1)S(1)}, u32[]{:S(2)}, u32[]{:S(2)}) collective-permute-start(bf16[256,128]{1,0:T(8,128)(2,1)} %param.6), channel_id=1, source_target_pairs={{0,16},{4,20},{8,24},{12,28},{16,32},{20,36},{24,40},{28,44},{32,4... | collective-permute-start | bytes 196616 | tf_op jit(solution)/shard_map/ppermute | solution.py:10
  73.7 16.0 collective-permute-start.1
  89.7 9.3 collective-permute-start.7
  91.7 7.4 collective-permute-start.6
  99.8 15.6 copy-start
  99.8 15.6 copy-start.2
  133.5 24.7 %collective-permute-start.15 = (bf16[256,128]{1,0:T(8,128)(2,1)S(1)}, bf16[256,128]{1,0:T(8,128)(2,1)S(1)}, u32[]{:S(2)}, u32[]{:S(2)}) collective-permute-start(bf16[256,128]{1,0:T(8,128)(2,1)S(1)} %bitcast.77), channel_id=1, source_target_pairs={{0,16},{4,20},{8,24},{12,28},{16,32},{20,36},{24,40},{28,44},{32,4... | collective-permute-start | bytes 196616 | tf_op jit(solution)/shard_map/ppermute | solution.py:10
  136.8 36.2 %collective-permute-start.8 = (bf16[256,128]{1,0:T(8,128)(2,1)S(1)}, bf16[256,128]{1,0:T(8,128)(2,1)S(1)}, u32[]{:S(2)}, u32[]{:S(2)}) collective-permute-start(bf16[256,128]{1,0:T(8,128)(2,1)S(1)} %bitcast.76), channel_id=1, source_target_pairs={{0,496},{4,500},{8,504},{12,508},{16,0},{20,4},{24,8},{28,12},{32,... | collective-permute-start | bytes 196616 | tf_op jit(solution)/shard_map/ppermute | solution.py:10
  148.1 28.0 %collective-permute-start.14 = (bf16[256,128]{1,0:T(8,128)(2,1)S(1)}, bf16[256,128]{1,0:T(8,128)(2,1)S(1)}, u32[]{:S(2)}, u32[]{:S(2)}) collective-permute-start(bf16[256,128]{1,0:T(8,128)(2,1)S(1)} %bitcast.75), channel_id=1, source_target_pairs={{0,12},{4,16},{8,20},{12,24},{16,28},{20,32},{24,36},{28,40},{32,4... | collective-permute-start | bytes 196616 | tf_op jit(solution)/shard_map/ppermute | solution.py:10
  153.2 27.8 %collective-permute-start.13 = (bf16[256,128]{1,0:T(8,128)(2,1)S(1)}, bf16[256,128]{1,0:T(8,128)(2,1)S(1)}, u32[]{:S(2)}, u32[]{:S(2)}) collective-permute-start(bf16[256,128]{1,0:T(8,128)(2,1)S(1)} %bitcast.74), channel_id=1, source_target_pairs={{0,8},{4,12},{8,16},{12,20},{16,24},{20,28},{24,32},{28,36},{32,40... | collective-permute-start | bytes 196616 | tf_op jit(solution)/shard_map/ppermute | solution.py:10
  156.3 24.7 %collective-permute-start.12 = (bf16[256,128]{1,0:T(8,128)(2,1)S(1)}, bf16[256,128]{1,0:T(8,128)(2,1)S(1)}, u32[]{:S(2)}, u32[]{:S(2)}) collective-permute-start(bf16[256,128]{1,0:T(8,128)(2,1)S(1)} %bitcast.73), channel_id=1, source_target_pairs={{0,4},{4,8},{8,12},{12,16},{16,20},{20,24},{24,28},{28,32},{32,36}... | collective-permute-start | bytes 196616 | tf_op jit(solution)/shard_map/ppermute | solution.py:10
  158.2 22.8 %collective-permute-start.11 = (bf16[256,128]{1,0:T(8,128)(2,1)S(1)}, bf16[256,128]{1,0:T(8,128)(2,1)S(1)}, u32[]{:S(2)}, u32[]{:S(2)}) collective-permute-start(bf16[256,128]{1,0:T(8,128)(2,1)S(1)} %bitcast.72), channel_id=1, source_target_pairs={{0,508},{4,0},{8,4},{12,8},{16,12},{20,16},{24,20},{28,24},{32,28}... | collective-permute-start | bytes 196616 | tf_op jit(solution)/shard_map/ppermute | solution.py:10
  173.0 8.0 collective-permute-start.10
  176.1 7.4 collective-permute-start.9
Sparse Core Ops, SparseCore 0:
  181.1 1839.3 all-reduce.1
where the time goes:
time: 2030 us
  waiting for transfers between devices  1860 us (92%)
  starting transfers between devices  75.2 us (4%)
  blocking collectives  71.7 us (4%)
    psum x1, waiting for transfers between devices, on_device(): grad_weight = lax.psum(weight_terms, 'rows') * float(node_total) ** (-0.5)  1840 us
    ppermute x16, starting transfers between devices, shifted(): return lax.ppermute(value, axis, pairs)  75.2 us
  transfers between devices with their start and end apart: 17, of which 4 were waited for; matrix products, arithmetic and copies ran while one was open for 0% of the time, Pallas kernels for 0%

commit v1 on v0

--- a/solution.py
+++ b/solution.py
@@ -73,7 +73,9 @@
         agg_full, grad_pre, (((0,), (0,)), ((), ())), preferred_element_type=jnp.float32
     )
     node_total = local_rows * row_count
-    grad_weight = lax.psum(weight_terms, "rows") * float(node_total) ** (-0.5)
+    grad_weight = jnp.sum(jax.lax.all_gather(weight_terms, "rows"), axis=0) * float(node_total) ** (
+        -0.5
+    )
     feat_index = lax.axis_index("feat")
     weight_rows = lax.dynamic_slice_in_dim(weight_full, feat_index * feat_width, feat_width, 0)
     grad_agg = lax.dot_general(

time: 2030 us -> 1130 us (0.56)
  waiting for transfers between devices: 1860 us -> 950 us
    psum x1 -> x0, waiting for transfers between devices: 1840 us -> none  [on_device(): grad_weight = lax.psum(weight_terms, 'rows') * float(node_total) ** (-0.5)]
    all_gather x0 -> x1, waiting for transfers between devices: none -> 942 us  [on_device(): jax.lax.all_gather(weight_terms, 'rows')]
  transfers between devices with their start and end apart: 17 -> 17, of which waited for: 4 -> 6; matrix products, arithmetic and copies ran while one was open for 0% -> 0% of each run, Pallas kernels for 0% -> 0%
where the time goes in v1:
time: 1130 us
  waiting for transfers between devices  950 us (84%)
  starting transfers between devices  72.2 us (6%)
  blocking collectives  72 us (6%)
  other arithmetic  16.5 us (1%)
  between operations  14.4 us (1%)
    all_gather x1, waiting for transfers between devices, on_device(): jax.lax.all_gather(weight_terms, 'rows')  942 us
    ppermute x16, starting transfers between devices, shifted(): return lax.ppermute(value, axis, pairs)  72.2 us
    all_gather x1, blocking collectives, on_device(): panel_full = lax.all_gather(block_values, 'feat', axis=1, tiled=True)  24.6 us
  transfers between devices with their start and end apart: 17, of which 6 were waited for; matrix products, arithmetic and copies ran while one was open for 0% of the time, Pallas kernels for 0%

profile of v1, /device:TPU:0, one launch (start us, length us, event | category | flops | bytes accessed | tf_op | source)
XLA Modules:
  0.0 1129.4 jit_solution(1902118900952483144)
XLA Ops:
  7.2 0.0 copy-start.1
  7.2 0.0 all-gather.3.cloned.1.call-start
  7.2 1.9 collective-permute-start
  9.2 1.9 collective-permute-start.1
  11.1 3.5 collective-permute-start.2
  14.5 2.9 collective-permute-start.3
  17.4 13.8 %collective-permute-start.4 = (bf16[256,128]{1,0:T(8,128)(2,1)}, bf16[256,128]{1,0:T(8,128)(2,1)S(1)}, u32[]{:S(2)}, u32[]{:S(2)}) collective-permute-start(bf16[256,128]{1,0:T(8,128)(2,1)} %param.6), channel_id=1, source_target_pairs={{0,508},{4,0},{8,4},{12,8},{16,12},{20,16},{24,20},{28,24},{32,28}... | collective-permute-start | bytes 196616 | tf_op jit(solution)/shard_map/ppermute | solution.py:10
  31.2 0.7 compare_and_fusion
  32.0 0.1 reshape.107
  32.0 24.6 %all_gather.18 = bf16[2,8,128,128]{3,2,1,0:T(8,128)(2,1)S(1)} all-gather(bf16[2,2,128,128]{3,2,1,0:T(8,128)(2,1)} %param.8), channel_id=1, replica_groups=mesh['rows'=128,'feat'=4] {'feat'}, dimensions={1}, use_global_device_ids=true | all-gather | bytes 655360 | tf_op jit(solution)/shard_map/all_gather | solution.py:61
  56.6 0.7 iota_compare_fusion
  57.4 0.0 collective-permute-done
  57.4 3.6 collective-permute-start.5
  61.0 0.0 collective-permute-done.1
  61.1 2.7 collective-permute-start.6
  63.8 0.0 collective-permute-done.2
  63.8 3.5 collective-permute-start.7
  67.3 0.0 collective-permute-done.3
  67.3 0.0 copy-done.1
  67.3 0.0 collective-permute-done.4
  67.4 0.0 collective-permute-done.5
  67.4 1.2 collective-permute-done.6
  68.7 1.5 collective-permute-done.7
  70.2 0.6 gather_fusion
  70.8 0.0 copy-start
  70.8 0.0 copy-start.2
  70.8 0.4 fusion
  71.2 14.9 %all_gather.19 = bf16[256,512]{1,0:T(8,128)(2,1)S(1)} all-gather(bf16[256,128]{1,0:T(8,128)(2,1)S(1)} %bitcast.80), channel_id=1, replica_groups=mesh['rows'=128,'feat'=4] {'feat'}, dimensions={1}, use_global_device_ids=true | all-gather | bytes 327680 | tf_op jit(solution)/shard_map/all_gather | solution.py:65
  86.1 0.0 copy-done
  86.1 0.0 copy-done.2
  86.1 0.9 fusion.9
  87.0 1.0 fusion.36
  88.0 0.0 all-gather.3.cloned.1.call-update
  88.0 0.1 reshape.102
  88.1 17.1 %all_gather.21 = bf16[512,512]{1,0:T(8,128)(2,1)S(1)} all-gather(bf16[512,128]{1,0:T(8,128)(2,1)S(1)} %copy-done), channel_id=1, replica_groups=mesh['rows'=128,'feat'=4] {'feat'}, dimensions={1}, use_global_device_ids=true | all-gather | bytes 655360 | tf_op jit(solution)/shard_map/all_gather | solution.py:66
  105.2 15.4 %all_gather.20 = bf16[256,512]{1,0:T(8,128)(2,1)S(1)} all-gather(bf16[256,128]{1,0:T(8,128)(2,1)S(1)} %get-tuple-element.13), channel_id=1, replica_groups=mesh['rows'=128,'feat'=4] {'feat'}, dimensions={1}, use_global_device_ids=true | all-gather | bytes 327680 | tf_op jit(solution)/shard_map/all_gather | solution.py:71
  120.6 0.2 convolution_convert_fusion
  120.9 0.4 fusion.3
  121.3 0.1 broadcast_in_dim.43
  121.4 1.6 scatter_fusion
  123.0 0.1 convert.10
  123.2 1.9 collective-permute-start.15
  125.1 7.3 collective-permute-start.14
  132.4 4.1 collective-permute-start.13
  136.6 3.6 collective-permute-start.12
  140.2 14.2 %collective-permute-start.11 = (bf16[256,128]{1,0:T(8,128)(2,1)S(1)}, bf16[256,128]{1,0:T(8,128)(2,1)S(1)}, u32[]{:S(2)}, u32[]{:S(2)}) collective-permute-start(bf16[256,128]{1,0:T(8,128)(2,1)S(1)} %bitcast.75), channel_id=1, source_target_pairs={{0,508},{4,0},{8,4},{12,8},{16,12},{20,16},{24,20},{28,24},{32,28}... | collective-permute-start | bytes 196616 | tf_op jit(solution)/shard_map/ppermute | solution.py:10
  154.4 0.0 collective-permute-done.15
  154.4 3.4 collective-permute-start.10
  157.8 0.0 collective-permute-done.14
  157.8 1.9 collective-permute-start.9
  159.7 0.0 collective-permute-done.13
  159.7 1.9 collective-permute-start.8
  161.7 0.0 collective-permute-done.12
  161.7 0.0 collective-permute-done.11
  161.7 0.6 collective-permute-done.10
  162.3 3.3 collective-permute-done.9
  165.5 1.2 collective-permute-done.8
  166.7 0.7 fusion.24
  167.4 942.4 %all-gather.3.cloned.1.call-done = f32[65536,128]{1,0:T(8,128)} async-done(((f32[512,128]{1,0:T(8,128)}), f32[65536,128]{1,0:T(8,128)}) %all-gather.3.cloned.1.call-update) | async-done | bytes 33554448 | tf_op jit(solution)/shard_map/all_gather | solution.py:76
  1109.8 12.0 %reduce_sum.9 = f32[512,128]{1,0:T(8,128)S(1)} reduce(f32[128,512,128]{2,1,0:T(8,128)} %bitcast.67, f32[]{:T(128)} %constant.84.clone.1), dimensions={0}, to_apply=%region_1.2 | reduce | flops 8323072 | bytes 33816580 | tf_op jit(solution)/shard_map/reduce_sum | solution.py:76
  1121.8 0.7 broadcast_multiply_fusion
  (14 shorter events, 0.2 us)
Async XLA Ops:
  7.2 60.2 %copy-start.1 = (bf16[256,128]{1,0:T(8,128)(2,1)S(1)}, bf16[256,128]{1,0:T(8,128)(2,1)}, u32[]{:S(2)}) copy-start(bf16[256,128]{1,0:T(8,128)(2,1)} %param.6) | copy-start | bytes 196612
  7.2 1102.7 %all-gather.3.cloned.1.call-start = ((), (), s32[]{:S(2)}) async-start(), calls=%async_computation | async-start | bytes 33816576 | tf_op jit(solution)/shard_map/all_gather | solution.py:76
  7.2 50.2 %collective-permute-start = (bf16[256,128]{1,0:T(8,128)(2,1)}, bf16[256,128]{1,0:T(8,128)(2,1)S(1)}, u32[]{:S(2)}, u32[]{:S(2)}) collective-permute-start(bf16[256,128]{1,0:T(8,128)(2,1)} %param.6), channel_id=1, source_target_pairs={{0,16},{4,20},{8,24},{12,28},{16,32},{20,36},{24,40},{28,44},{32,4... | collective-permute-start | bytes 196616 | tf_op jit(solution)/shard_map/ppermute | solution.py:10
  9.2 51.9 %collective-permute-start.1 = (bf16[256,128]{1,0:T(8,128)(2,1)}, bf16[256,128]{1,0:T(8,128)(2,1)S(1)}, u32[]{:S(2)}, u32[]{:S(2)}) collective-permute-start(bf16[256,128]{1,0:T(8,128)(2,1)} %param.6), channel_id=1, source_target_pairs={{0,12},{4,16},{8,20},{12,24},{16,28},{20,32},{24,36},{28,40},{32,4... | collective-permute-start | bytes 196616 | tf_op jit(solution)/shard_map/ppermute | solution.py:10
  11.1 52.7 %collective-permute-start.2 = (bf16[256,128]{1,0:T(8,128)(2,1)}, bf16[256,128]{1,0:T(8,128)(2,1)S(1)}, u32[]{:S(2)}, u32[]{:S(2)}) collective-permute-start(bf16[256,128]{1,0:T(8,128)(2,1)} %param.6), channel_id=1, source_target_pairs={{0,8},{4,12},{8,16},{12,20},{16,24},{20,28},{24,32},{28,36},{32,40... | collective-permute-start | bytes 196616 | tf_op jit(solution)/shard_map/ppermute | solution.py:10
  14.5 52.7 %collective-permute-start.3 = (bf16[256,128]{1,0:T(8,128)(2,1)}, bf16[256,128]{1,0:T(8,128)(2,1)S(1)}, u32[]{:S(2)}, u32[]{:S(2)}) collective-permute-start(bf16[256,128]{1,0:T(8,128)(2,1)} %param.6), channel_id=1, source_target_pairs={{0,4},{4,8},{8,12},{12,16},{16,20},{20,24},{24,28},{28,32},{32,36}... | collective-permute-start | bytes 196616 | tf_op jit(solution)/shard_map/ppermute | solution.py:10
  17.4 49.9 %collective-permute-start.4 = (bf16[256,128]{1,0:T(8,128)(2,1)}, bf16[256,128]{1,0:T(8,128)(2,1)S(1)}, u32[]{:S(2)}, u32[]{:S(2)}) collective-permute-start(bf16[256,128]{1,0:T(8,128)(2,1)} %param.6), channel_id=1, source_target_pairs={{0,508},{4,0},{8,4},{12,8},{16,12},{20,16},{24,20},{28,24},{32,28}... | collective-permute-start | bytes 196616 | tf_op jit(solution)/shard_map/ppermute | solution.py:10
  57.4 10.0 collective-permute-start.5
  61.1 7.6 collective-permute-start.6
  63.8 6.4 collective-permute-start.7
  70.8 15.3 %copy-start = (bf16[512,128]{1,0:T(8,128)(2,1)S(1)}, bf16[512,128]{1,0:T(8,128)(2,1)}, u32[]{:S(2)}) copy-start(bf16[512,128]{1,0:T(8,128)(2,1)} %param.7) | copy-start | bytes 393220
  70.8 15.3 %copy-start.2 = (bf16[256,128]{1,0:T(8,128)(2,1)S(1)}, bf16[256,128]{1,0:T(8,128)(2,1)}, u32[]{:S(2)}) copy-start(bf16[256,128]{1,0:T(8,128)(2,1)} %param.11) | copy-start | bytes 196612
  123.2 31.2 %collective-permute-start.15 = (bf16[256,128]{1,0:T(8,128)(2,1)S(1)}, bf16[256,128]{1,0:T(8,128)(2,1)S(1)}, u32[]{:S(2)}, u32[]{:S(2)}) collective-permute-start(bf16[256,128]{1,0:T(8,128)(2,1)S(1)} %bitcast.79), channel_id=1, source_target_pairs={{0,16},{4,20},{8,24},{12,28},{16,32},{20,36},{24,40},{28,44},{32,4... | collective-permute-start | bytes 196616 | tf_op jit(solution)/shard_map/ppermute | solution.py:10
  125.1 32.7 %collective-permute-start.14 = (bf16[256,128]{1,0:T(8,128)(2,1)S(1)}, bf16[256,128]{1,0:T(8,128)(2,1)S(1)}, u32[]{:S(2)}, u32[]{:S(2)}) collective-permute-start(bf16[256,128]{1,0:T(8,128)(2,1)S(1)} %bitcast.78), channel_id=1, source_target_pairs={{0,12},{4,16},{8,20},{12,24},{16,28},{20,32},{24,36},{28,40},{32,4... | collective-permute-start | bytes 196616 | tf_op jit(solution)/shard_map/ppermute | solution.py:10
  132.4 27.3 %collective-permute-start.13 = (bf16[256,128]{1,0:T(8,128)(2,1)S(1)}, bf16[256,128]{1,0:T(8,128)(2,1)S(1)}, u32[]{:S(2)}, u32[]{:S(2)}) collective-permute-start(bf16[256,128]{1,0:T(8,128)(2,1)S(1)} %bitcast.77), channel_id=1, source_target_pairs={{0,8},{4,12},{8,16},{12,20},{16,24},{20,28},{24,32},{28,36},{32,40... | collective-permute-start | bytes 196616 | tf_op jit(solution)/shard_map/ppermute | solution.py:10
  136.6 25.1 %collective-permute-start.12 = (bf16[256,128]{1,0:T(8,128)(2,1)S(1)}, bf16[256,128]{1,0:T(8,128)(2,1)S(1)}, u32[]{:S(2)}, u32[]{:S(2)}) collective-permute-start(bf16[256,128]{1,0:T(8,128)(2,1)S(1)} %bitcast.76), channel_id=1, source_target_pairs={{0,4},{4,8},{8,12},{12,16},{16,20},{20,24},{24,28},{28,32},{32,36}... | collective-permute-start | bytes 196616 | tf_op jit(solution)/shard_map/ppermute | solution.py:10
  140.2 21.5 %collective-permute-start.11 = (bf16[256,128]{1,0:T(8,128)(2,1)S(1)}, bf16[256,128]{1,0:T(8,128)(2,1)S(1)}, u32[]{:S(2)}, u32[]{:S(2)}) collective-permute-start(bf16[256,128]{1,0:T(8,128)(2,1)S(1)} %bitcast.75), channel_id=1, source_target_pairs={{0,508},{4,0},{8,4},{12,8},{16,12},{20,16},{24,20},{28,24},{32,28}... | collective-permute-start | bytes 196616 | tf_op jit(solution)/shard_map/ppermute | solution.py:10
  154.4 7.9 collective-permute-start.10
  157.8 7.7 collective-permute-start.9
  159.7 7.0 collective-permute-start.8
Sparse Core Ops, SparseCore 0:
  88.1 1021.6 all-gather.2
